TPU v7x, 32 devices: a whole 2x2x4 slice. The times are simulated.
32 devices in a mesh: row: 8 (over z, x), col: 4 (over y, core).
Axes of the slice: x: 2, y: 2, z: 4, core: 2. Of those that a mesh axis runs over, the one named last changes fastest.
Arguments:
- receptance: bfloat16 [2, 16384, 16384], P(None, 'row', 'col'), may hold values from -4 to 60, as said below
- coupling: int32 [2, 768], replicated, may hold values from 0 to 16383, as said below
Outputs:
- coupled: bfloat16 [2, 16384, 16384], P(None, 'row', 'col')
Inputs may be any that keep to these rules, and one draw needn't show every extreme that they name: `coupling`: row 0 holds 768 distinct body DOFs, all in the first half of the 16384 DOFs; row 1 holds 768 distinct cavity DOFs, all in the second half. `receptance`: the driving-point entry of every body or cavity DOF named in coupling (same response and excitation DOF) has real part 52 or more; every other real or imaginary part lies within -4 to 4.
All inputs are finite; a program needn't handle non-finite values.
Results may differ from a plain program's by a relative error of at most 0.015.
Values may be sent and summed in bfloat16 or wider, within the bound.
A program may use at most 320 MiB of HBM per device.

v0:
```python
import jax
import jax.numpy as jnp
from jax import lax
from jax.sharding import PartitionSpec as P

SWEEPS = 6


def select_rows(matrix, body_dof, cav_dof, offset, extent):
    count = body_dof.shape[0]
    both_dof = jnp.concatenate([body_dof, cav_dof]) - offset
    inside = (both_dof >= 0) & (both_dof < extent)
    clipped = jnp.clip(both_dof, 0, extent - 1)
    picked = jnp.take(matrix, clipped, axis=1).astype(jnp.float32)
    picked = jnp.where(inside[None, :, None], picked, jnp.zeros((), jnp.float32))
    return picked[:, :count, :] - picked[:, count:, :]


def select_columns(matrix, body_dof, cav_dof, offset, extent):
    positions = offset + lax.broadcasted_iota(jnp.int32, (extent, 1), 0)
    table = (positions == body_dof[None, :]).astype(jnp.float32) - (
        positions == cav_dof[None, :]
    ).astype(jnp.float32)
    table = table.astype(matrix.dtype)
    return jnp.einsum(
        "prc,cn->prn",
        matrix,
        table,
        preferred_element_type=jnp.float32,
        precision=lax.Precision.HIGHEST,
    )


def complex_times(mat_real, mat_imag, vec_real, vec_imag):
    hi = lax.Precision.HIGHEST
    out_real = jnp.dot(mat_real, vec_real, precision=hi) - jnp.dot(mat_imag, vec_imag, precision=hi)
    out_imag = jnp.dot(mat_real, vec_imag, precision=hi) + jnp.dot(mat_imag, vec_real, precision=hi)
    return (out_real, out_imag)


def local(receptance, coupling):
    tile_rows = receptance.shape[1]
    tile_cols = receptance.shape[2]
    row_index = lax.axis_index("row")
    col_index = lax.axis_index("col")
    body_dof = coupling[0]
    cav_dof = coupling[1]
    row_terms = select_rows(receptance, body_dof, cav_dof, row_index * tile_rows, tile_rows)
    rhs_local = lax.psum_scatter(
        row_terms.astype(jnp.bfloat16), "row", scatter_dimension=2, tiled=True
    ).astype(jnp.float32)
    solve_cols = rhs_local.shape[2]
    column_terms = select_columns(receptance, body_dof, cav_dof, col_index * tile_cols, tile_cols)
    left_full = lax.psum(column_terms.astype(jnp.bfloat16), "col")
    first_col = col_index * tile_cols + row_index * solve_cols
    inter_terms = select_columns(rhs_local, body_dof, cav_dof, first_col, solve_cols)
    interface = lax.psum(inter_terms, ("row", "col"))
    z_real = interface[0]
    z_imag = interface[1]
    diag_real = jnp.diagonal(z_real)
    diag_imag = jnp.diagonal(z_imag)
    modulus = diag_real * diag_real + diag_imag * diag_imag
    d_real = (diag_real / modulus)[:, None]
    d_imag = (-diag_imag / modulus)[:, None]

    def scale(part_real, part_imag):
        return (d_real * part_real - d_imag * part_imag, d_real * part_imag + d_imag * part_real)

    v_real = rhs_local[0]
    v_imag = rhs_local[1]
    x_real, x_imag = scale(v_real, v_imag)
    for sweep_index in range(SWEEPS):
        p_real, p_imag = complex_times(z_real, z_imag, x_real, x_imag)
        e_real, e_imag = scale(v_real - p_real, v_imag - p_imag)
        x_real = x_real + e_real
        x_imag = x_imag + e_imag
    weights = jnp.stack([x_real, x_imag]).astype(jnp.bfloat16)
    u_real = left_full[0]
    u_imag = left_full[1]
    column_piece = lax.all_gather(weights, "row", axis=2, tiled=True)
    p_real = column_piece[0]
    p_imag = column_piece[1]
    c_real = jnp.dot(u_real, p_real, preferred_element_type=jnp.float32) - jnp.dot(
        u_imag, p_imag, preferred_element_type=jnp.float32
    )
    c_imag = jnp.dot(u_real, p_imag, preferred_element_type=jnp.float32) + jnp.dot(
        u_imag, p_real, preferred_element_type=jnp.float32
    )
    recv_piece = receptance.astype(jnp.float32)
    return (recv_piece - jnp.stack([c_real, c_imag])).astype(jnp.bfloat16)


def solution(mesh):
    in_specs = (P(None, "row", "col"), P())
    out_specs = P(None, "row", "col")
    return jax.shard_map(local, mesh=mesh, in_specs=in_specs, out_specs=out_specs, check_vma=False)
```

profile of v0, /device:TPU:0, one launch (start us, length us, event | category | flops | bytes accessed | tf_op | source)
XLA Modules:
  0.0 973.7 jit_solution(2592334917314808475)
XLA Ops:
  7.4 93.8 %gather_fusion = bf16[1536,2,4096]{2,0,1:T(8,128)(2,1)} fusion(bf16[2,2048,4096]{2,1,0:T(8,128)(2,1)} %param.2, s32[2048]{0:T(1024)S(1)} %pad_clamp_fusion), kind=kCustom, calls=%fused_computation | custom fusion | bytes 50337792 | tf_op jit(solution)/shard_map/jit(_take)/gather | solution.py:14
  101.2 27.7 %select_bitcast_fusion = f32[2,1536,4096]{2,1,0:T(8,128)} fusion(bf16[1536,2,4096]{2,0,1:T(8,128)(2,1)} %gather_fusion, pred[1536]{0:T(1024)(128)(4,1)S(1)} %get-tuple-element.24, pred[1536]{0:T(1024)(128)(4,1)S(1)} %get-tuple-element.23), kind=kLoop, calls=%fused_computation.5 | loop fusion | flops 37748736 | bytes 75500544 | tf_op jit(solution)/shard_map/jit(_where)/select_n | solution.py:15
  128.9 21.2 %fusion.1 = bf16[2,768,4096]{2,1,0:T(8,128)(2,1)} fusion(f32[2,1536,4096]{2,1,0:T(8,128)} %select_bitcast_fusion), kind=kLoop, calls=%fused_computation.9 | loop fusion | flops 12582912 | bytes 62914560 | tf_op jit(solution)/shard_map/convert_element_type | solution.py:50
  150.2 207.2 %reduce-scatter.2.cloned.1.call-done = bf16[2,768,512]{2,1,0:T(8,128)(2,1)} async-done(((bf16[2,768,4096]{2,1,0:T(8,128)(2,1)}), bf16[2,768,512]{2,1,0:T(8,128)(2,1)}) %reduce-scatter.2.cloned.1.call-update) | async-done | bytes 1572880 | tf_op jit(solution)/shard_map/reduce_scatter | solution.py:49
  357.4 7.8 fusion.24
  365.3 31.4 %convert_bitcast_fusion = bf16[2,2048,768]{1,2,0:T(8,128)(2,1)} fusion(bf16[2,2048,4096]{2,1,0:T(8,128)(2,1)} %param.2, s32[4096]{0:T(1024)S(1)} %iota_add_fusion, s32[768]{0:T(1024)S(1)} %get-tuple-element.6, s32[768]{0:T(1024)S(1)} %get-tuple-element.5), kind=kOutput, calls=%fused_computation.15 | convolution fusion | flops 25791823872 | bytes 39868416 | tf_op jit(solution)/shard_map/prc,cn->prn/dot_general | solution.py:25
  400.2 109.1 %all-reduce.5.cloned.1.call-done = f32[2,768,768]{2,1,0:T(8,128)} async-done(((f32[2,768,768]{2,1,0:T(8,128)}), f32[2,768,768]{2,1,0:T(8,128)}) %all-reduce.5.cloned.1.call-update) | async-done | bytes 4718608 | tf_op jit(solution)/shard_map/psum | solution.py:57
  513.5 12.4 %gather_fusion.1 = f32[768]{0:T(1024)S(1)} fusion(f32[768,768]{1,0:T(8,128)} %get-tuple-element.9, s32[768]{0:T(1024)S(1)} %or_reduce_fusion), kind=kCustom, calls=%fused_computation.1 | custom fusion | bytes 12288 | tf_op jit(solution)/shard_map/jit(diagonal)/cond/branch_0_fun/gather | solution.py:60
  525.9 6.5 gather_fusion.2
  532.4 6.9 fusion.12
  539.3 6.9 fusion.14
  550.5 5.1 fusion.21
  567.3 4.8 subtract_add_fusion.3
  583.8 4.5 subtract_add_fusion.2
  600.3 4.3 subtract_add_fusion.1
  612.4 4.4 bitcast_subtract_fusion.7
  616.8 4.3 subtract_add_fusion
  633.1 4.5 fusion.35
  638.9 175.8 %all-gather.2.cloned.1.call-done = bf16[2,768,4096]{2,1,0:T(8,128)(2,1)} async-done(((bf16[2,768,512]{2,1,0:T(8,128)(2,1)}), bf16[2,768,4096]{2,1,0:T(8,128)(2,1)}) %all-gather.2.cloned.1.call-update) | async-done | bytes 12582928 | tf_op jit(solution)/shard_map/all_gather | solution.py:80
  814.7 23.2 %fusion.9 = f32[2048,4096]{1,0:T(8,128)} fusion(bf16[2,768,4096]{2,1,0:T(8,128)(2,1)} %all-gather.2.cloned.1.call-done, bf16[2,2048,768]{1,2,0:T(8,128)(2,1)} %all-reduce.3.cloned.1.call-done), kind=kOutput, calls=%fused_computation.20 | convolution fusion | flops 12884901888 | bytes 42991616 | tf_op jit(solution)/shard_map/dot_general | solution.py:86
  838.0 20.2 %fusion.8 = f32[2048,4096]{1,0:T(8,128)} fusion(bf16[2,768,4096]{2,1,0:T(8,128)(2,1)} %all-gather.2.cloned.1.call-done, bf16[2,2048,768]{1,2,0:T(8,128)(2,1)S(1)} %copy-done.2), kind=kOutput, calls=%fused_computation.19 | convolution fusion | flops 12884901888 | bytes 42991616 | tf_op jit(solution)/shard_map/dot_general | solution.py:83
  858.2 33.0 %add_bitcast_fusion = f32[1,2048,4096]{2,1,0:T(8,128)} fusion(f32[2048,4096]{1,0:T(8,128)} %fusion.9, bf16[2,768,4096]{2,1,0:T(8,128)(2,1)} %all-gather.2.cloned.1.call-done, bf16[2,2048,768]{1,2,0:T(8,128)(2,1)} %all-reduce.3.cloned.1.call-done), kind=kOutput, calls=%fused_computation.6 | convolution fusion | flops 12893290496 | bytes 76546048 | tf_op jit(solution)/shard_map/dot_general | solution.py:86
  891.1 33.3 %subtract_bitcast_fusion = f32[1,2048,4096]{2,1,0:T(8,128)} fusion(f32[2048,4096]{1,0:T(8,128)} %fusion.8, bf16[2,768,4096]{2,1,0:T(8,128)(2,1)} %all-gather.2.cloned.1.call-done, bf16[2,2048,768]{1,2,0:T(8,128)(2,1)} %all-reduce.3.cloned.1.call-done), kind=kOutput, calls=%fused_computation.7 | convolution fusion | flops 12893290496 | bytes 76546048 | tf_op jit(solution)/shard_map/dot_general | solution.py:83
  924.4 42.3 %fusion = bf16[2,2048,4096]{2,1,0:T(8,128)(2,1)} fusion(f32[1,2048,4096]{2,1,0:T(8,128)} %add_bitcast_fusion, f32[1,2048,4096]{2,1,0:T(8,128)} %subtract_bitcast_fusion, bf16[2,2048,4096]{2,1,0:T(8,128)(2,1)} %param.2), kind=kLoop, calls=%fused_computation.4 | loop fusion | flops 67108864 | bytes 134217728 | tf_op jit(solution)/shard_map/convert_element_type | solution.py:90
  (46 shorter events, 69.2 us)
Async XLA Ops:
  6.5 350.9 %reduce-scatter.2.cloned.1.call-start = ((), (), s32[]{:S(2)}) async-start(), calls=%async_computation.2 | async-start | bytes 14155776 | tf_op jit(solution)/shard_map/reduce_scatter | solution.py:49
  150.1 359.3 %all-reduce.5.cloned.1.call-start = ((), (), s32[]{:S(2)}) async-start(), calls=%async_computation.3 | async-start | bytes 9437184 | tf_op jit(solution)/shard_map/psum | solution.py:57
  365.3 273.6 %all-reduce.3.cloned.1.call-start = ((), (), s32[]{:S(2)}) async-start(), calls=%async_computation.1 | async-start | bytes 12582912 | tf_op jit(solution)/shard_map/psum | solution.py:54
  396.7 1.4 copy-start.1
  396.7 418.0 %all-gather.2.cloned.1.call-start = ((), (), s32[]{:S(2)}) async-start(), calls=%async_computation.4 | async-start | bytes 14155776 | tf_op jit(solution)/shard_map/all_gather | solution.py:80
  525.9 20.3 %slice-start = ((s8[4718592]{0:T(1024)(128)(4,1)}), s8[524288]{0:T(1024)(128)(4,1)S(1)}, s32[]{:S(2)}) async-start(s8[4718592]{0:T(1024)(128)(4,1)} %bitcast.150), calls=%async_computation.5 | async-start | bytes 1048576
  532.4 13.8 %slice-start.1 = ((s8[4718592]{0:T(1024)(128)(4,1)}), s8[4194304]{0:T(1024)(128)(4,1)S(1)}, s32[]{:S(2)}) async-start(s8[4718592]{0:T(1024)(128)(4,1)} %bitcast.150), calls=%async_computation.6 | async-start | bytes 8388608
  539.3 6.9 copy-start
  814.7 23.2 %copy-start.2 = (bf16[2,2048,768]{1,2,0:T(8,128)(2,1)S(1)}, bf16[2,2048,768]{1,2,0:T(8,128)(2,1)}, u32[]{:S(2)}) copy-start(bf16[2,2048,768]{1,2,0:T(8,128)(2,1)} %all-reduce.3.cloned.1.call-done) | copy-start | bytes 18874372
Sparse Core Ops, SparseCore 0:
  150.2 207.1 reduce-scatter.1
  365.4 143.9 all-reduce.4
  511.9 118.4 all-reduce.2
  639.0 175.6 all-gather.1
where the time goes:
time: 985 us; the launch traced here: 974 us
  waiting for transfers between devices  492 us (50%)
  matrix products  254 us (26%)
  local copies, waits for them, and re-layouts  119 us (12%)
  other arithmetic  94.7 us (10%)
  between operations  13.9 us (1%)
    reduce_scatter x1, waiting for transfers between devices, local(): lax.psum_scatter(row_terms.astype(jnp.bfloat16), 'row', scatter_dimension...  207 us
    all_gather x1, waiting for transfers between devices, local(): column_piece = lax.all_gather(weights, 'row', axis=2, tiled=True)  176 us
    psum x1, waiting for transfers between devices, local(): interface = lax.psum(inter_terms, ('row', 'col'))  109 us
    gather x1, local copies, waits for them, and re-layouts, select_rows(): picked = jnp.take(matrix, clipped, axis=1).astype(jnp.float32)  93.8 us
    convert_element_type x1, other arithmetic, local(): return (recv_piece - jnp.stack([c_real, c_imag])).astype(jnp.bfloat16)  42.3 us
    dot_general x2, matrix products, select_columns(): jnp.einsum('prc,cn->prn', matrix, table, preferred_element_type=jnp.float...  39.2 us
    dot_general x1, matrix products, local(): jnp.dot(u_imag, p_imag, preferred_element_type=jnp.float32)  33.3 us
    dot_general x1, matrix products, local(): jnp.dot(u_imag, p_real, preferred_element_type=jnp.float32)  33 us
  transfers between devices with their start and end apart: 4, of which 3 were waited for; matrix products, arithmetic and copies ran while one was open for 17% of the time, Pallas kernels for 0%

commit v1 on v0

v1 whole, which is shorter than its diff:
```python
import functools

import jax
import jax.numpy as jnp
from jax import lax
from jax.experimental import pallas as pl
from jax.experimental.pallas import tpu as pltpu
from jax.sharding import PartitionSpec as P

BF = jnp.bfloat16
F32 = jnp.float32


def signed_table(body_dof, cav_dof, offset, extent):
    positions = offset + lax.broadcasted_iota(jnp.int32, (extent, 1), 0)
    table = (positions == body_dof[None, :]).astype(F32) - (positions == cav_dof[None, :]).astype(F32)
    return table.astype(BF)


def signed_table_t(body_dof, cav_dof, offset, extent):
    positions = offset + lax.broadcasted_iota(jnp.int32, (1, extent), 1)
    table = (positions == body_dof[:, None]).astype(F32) - (positions == cav_dof[:, None]).astype(F32)
    return table.astype(BF)


def sum_over_col(x, size):
    if size < 2 or size & (size - 1) or x.shape[1] % 32:
        return lax.psum(x, "col")
    half = x.shape[1] // 2
    me = lax.axis_index("col")
    bit = me % 2
    pair = [(i, i ^ 1) for i in range(size)]
    mine = lax.dynamic_slice_in_dim(x, bit * half, half, 1)
    other = lax.dynamic_slice_in_dim(x, (1 - bit) * half, half, 1)
    mine = mine + lax.ppermute(other, "col", pair)
    step = 2
    while step < size:
        mine = mine + lax.ppermute(mine, "col", [(i, i ^ step) for i in range(size)])
        step *= 2
    other = lax.ppermute(mine, "col", pair)
    low = jnp.where(bit == 0, mine, other)
    high = jnp.where(bit == 0, other, mine)
    return jnp.concatenate([low, high], axis=1)


def final_kernel(first, *refs):
    if first:
        y_ref, u_ref, w_ref, o_ref = refs
    else:
        y_ref, u_ref, w_ref, _, o_ref = refs
    for p in range(2):
        c = jnp.dot(u_ref[p], w_ref[...], preferred_element_type=F32)
        o_ref[p] = (y_ref[p].astype(F32) - c).astype(BF)


def final_chunk(y, u, w, prev, index):
    _, rows, cols = y.shape
    depth, width = w.shape
    bm = min(512, rows)
    bn = min(1024, width)
    base = index * (width // bn)
    first = prev is None
    in_specs = [
        pl.BlockSpec((2, bm, bn), lambda j, i: (0, i, base + j)),
        pl.BlockSpec((2, bm, depth), lambda j, i: (0, i, 0)),
        pl.BlockSpec((depth, bn), lambda j, i: (0, j)),
    ]
    args = [y, u, w]
    aliases = {}
    if not first:
        in_specs.append(pl.BlockSpec(memory_space=pl.ANY))
        args.append(prev)
        aliases = {3: 0}
    return pl.pallas_call(
        functools.partial(final_kernel, first),
        grid=(width // bn, rows // bm),
        in_specs=in_specs,
        out_specs=pl.BlockSpec((2, bm, bn), lambda j, i: (0, i, base + j)),
        out_shape=jax.ShapeDtypeStruct(y.shape, BF),
        input_output_aliases=aliases,
        compiler_params=pltpu.CompilerParams(vmem_limit_bytes=48 * 1024 * 1024),
        cost_estimate=pl.CostEstimate(
            flops=4 * rows * depth * width,
            bytes_accessed=8 * rows * width + 4 * rows * depth + 2 * depth * width,
            transcendentals=0,
        ),
    )(*args)


def times(a_r, a_i, b_r, b_i, precision=lax.Precision.HIGH):
    left = jnp.concatenate([a_r, a_i], axis=1)
    right = jnp.concatenate(
        [jnp.concatenate([b_r, b_i], axis=1), jnp.concatenate([-b_i, b_r], axis=1)], axis=0
    )
    out = jnp.dot(left, right, precision=precision, preferred_element_type=F32)
    n = b_r.shape[1]
    return out[:, :n], out[:, n:]


def solve_operator(z_real, z_imag):
    n = z_real.shape[0]
    eye = lax.broadcasted_iota(jnp.int32, (n, n), 0) == lax.broadcasted_iota(jnp.int32, (n, n), 1)
    zero = jnp.zeros((), F32)

    def inverse(axis):
        re = jnp.sum(jnp.where(eye, z_real, zero), axis=axis, keepdims=True)
        im = jnp.sum(jnp.where(eye, z_imag, zero), axis=axis, keepdims=True)
        modulus = re * re + im * im
        return re / modulus, -im / modulus

    d_r, d_i = inverse(1)
    o_r = jnp.where(eye, zero, z_real)
    o_i = jnp.where(eye, zero, z_imag)
    a_r = -(d_r * o_r - d_i * o_i)
    a_i = -(d_r * o_i + d_i * o_r)
    s_r, s_i = times(a_r, a_i, a_r, a_i)
    q_r, q_i = times(s_r, s_i, s_r, s_i)
    one = eye.astype(F32)
    p_r, p_i = times(a_r + s_r, a_i + s_i, one + s_r + q_r, s_i + q_i)
    p_r = p_r + one
    e_r, e_i = inverse(0)
    w_r = p_r * e_r - p_i * e_i
    w_i = p_r * e_i + p_i * e_r
    first = jnp.concatenate(
        [jnp.concatenate([w_r, -w_i], axis=1), jnp.concatenate([-w_i, -w_r], axis=1)], axis=0
    )
    second = jnp.concatenate(
        [jnp.concatenate([w_i, w_r], axis=1), jnp.concatenate([w_r, -w_i], axis=1)], axis=0
    )
    return jnp.stack([first, second]).astype(BF)


def local(row_size, col_size, receptance, coupling):
    _, tile_rows, tile_cols = receptance.shape
    row_index = lax.axis_index("row")
    col_index = lax.axis_index("col")
    body_dof = coupling[0]
    cav_dof = coupling[1]
    count = body_dof.shape[0]
    col_table = signed_table(body_dof, cav_dof, col_index * tile_cols, tile_cols)
    row_table = signed_table_t(body_dof, cav_dof, row_index * tile_rows, tile_rows)

    chunks = 4 if tile_cols % 512 == 0 else 1
    width = tile_cols // chunks

    def row_chunk(j, table):
        part = receptance[:, :, j * width : (j + 1) * width]
        terms = jnp.einsum("nr,prc->pnc", table, part, preferred_element_type=F32).astype(BF)
        return terms.reshape(2 * count, width)

    def scatter(terms):
        return lax.psum_scatter(terms, "row", scatter_dimension=0, tiled=True)

    rows = row_chunk(0, row_table)
    col_table, rows = lax.optimization_barrier((col_table, rows))
    scattered = [scatter(rows)]
    col_terms = jnp.einsum("prc,cn->prn", receptance, col_table, preferred_element_type=F32).astype(BF)
    inter_terms = jnp.einsum("mr,prn->pmn", row_table, col_terms, preferred_element_type=F32).astype(BF)
    interface = lax.psum(inter_terms, ("row", "col"))
    scattered += [scatter(row_chunk(j, row_table)) for j in range(1, chunks)]
    left = sum_over_col(col_terms, col_size)
    z = interface.astype(F32)
    pages = solve_operator(z[0], z[1])
    left = jnp.concatenate([left[0], left[1]], axis=1)
    u = jnp.einsum("rk,pkn->prn", left, pages, preferred_element_type=F32).astype(BF)
    out = None
    for j in range(chunks):
        piece = lax.all_gather(scattered[j], "row", axis=0, tiled=True)
        out = final_chunk(receptance, u, piece, out, j)
    return out


def solution(mesh):
    in_specs = (P(None, "row", "col"), P())
    out_specs = P(None, "row", "col")
    body = functools.partial(local, mesh.shape["row"], mesh.shape["col"])
    return jax.shard_map(body, mesh=mesh, in_specs=in_specs, out_specs=out_specs, check_vma=False)
```

time: 985 us -> 626 us (0.64)
  waiting for transfers between devices: 492 us -> 281 us
  local copies, waits for them, and re-layouts: 119 us -> 20.6 us
  matrix products: 254 us -> 168 us
  Pallas kernels: 0 us -> 70.8 us
  other arithmetic: 94.7 us -> 61.7 us
    gather x3 -> x0, local copies, waits for them, and re-layouts: 113 us -> none  [the longest x1 93.8 us: select_rows(): picked = jnp.take(matrix, clipped, axis=1).astype(jnp.float32)]
    reduce_scatter x1 -> x4, waiting for transfers between devices: 207 us -> 105 us  [scatter(): return lax.psum_scatter(terms, 'row', scatter_dimension=0, tiled=True)]
    dot_general x30 -> x10, matrix products: 254 us -> 168 us  [the longest x3 62 us: times(): out = jnp.dot(left, right, precision=precision, preferred_element_type=F32)]
    pallas_call x0 -> x4, Pallas kernels: none -> 70.8 us  [final_chunk(): pl.pallas_call(functools.partial(final_kernel, first), grid=(width // bn,...]
    convert_element_type x3 -> x2, other arithmetic: 65.6 us -> 6.67 us  [the longest x1 4.65 us: signed_table(): return table.astype(BF)]
    psum x1, waiting for transfers between devices: 109 us -> 52.9 us  [local(): interface = lax.psum(inter_terms, ('row', 'col'))]
    all_gather x1 -> x4, waiting for transfers between devices: 176 us -> 122 us  [local(): piece = lax.all_gather(scattered[j], 'row', axis=0, tiled=True)]
    select_n x2 -> x1, other arithmetic: 27.7 us -> 3.4 us  [sum_over_col(): low = jnp.where(bit == 0, mine, other)]
  transfers between devices with their start and end apart: 4 -> 12, of which waited for: 3 -> 7; matrix products, arithmetic and copies ran while one was open for 17% -> 36% of each run, Pallas kernels for 0% -> 9%
where the time goes in v1:
time: 626 us; the launch traced here: 621 us
  waiting for transfers between devices  281 us (45%)
  matrix products  168 us (27%)
  Pallas kernels  70.8 us (11%)
  other arithmetic  61.7 us (10%)
  local copies, waits for them, and re-layouts  20.6 us (3%)
  between operations  15.7 us (3%)
    all_gather x4, waiting for transfers between devices, local(): piece = lax.all_gather(scattered[j], 'row', axis=0, tiled=True)  122 us
    reduce_scatter x4, waiting for transfers between devices, scatter(): return lax.psum_scatter(terms, 'row', scatter_dimension=0, tiled=True)  105 us
    pallas_call x4, Pallas kernels, final_chunk(): pl.pallas_call(functools.partial(final_kernel, first), grid=(width // bn,...  70.8 us
    dot_general x3, matrix products, times(): out = jnp.dot(left, right, precision=precision, preferred_element_type=F32)  62 us
    psum x1, waiting for transfers between devices, local(): interface = lax.psum(inter_terms, ('row', 'col'))  52.9 us
    dot_general x4, matrix products, row_chunk(): jnp.einsum('nr,prc->pnc', table, part, preferred_element_type=F32)  41.5 us
    dot_general x1, matrix products, local(): jnp.einsum('prc,cn->prn', receptance, col_table, preferred_element_type=F32)  32 us
    dot_general x1, matrix products, local(): jnp.einsum('rk,pkn->prn', left, pages, preferred_element_type=F32)  26.2 us
  transfers between devices with their start and end apart: 12, of which 7 were waited for; matrix products, arithmetic and copies ran while one was open for 36% of the time, Pallas kernels for 9%

profile of v1, /device:TPU:0, one launch (start us, length us, event | category | flops | bytes accessed | tf_op | source)
XLA Modules:
  0.0 620.8 jit_solution(2292988883400132463)
XLA Ops:
  12.8 10.3 %fusion.77 = bf16[768,2,1024]{2,0,1:T(8,128)(2,1)} fusion(bf16[2,2048,4096]{2,1,0:T(8,128)(2,1)} %refs_0_.7, s32[2048]{0:T(1024)S(1)} %iota_add_fusion.1, s32[768]{0:T(1024)S(1)} %get-tuple-element.14, s32[768]{0:T(1024)S(1)} %get-tuple-element.13), kind=kOutput, calls=%fused_computation.96 | convolution fusion | flops 6453460992 | bytes 11548672 | tf_op jit(solution)/shard_map/nr,prc->pnc/dot_general | solution.py:148
  23.2 10.4 %fusion.92 = bf16[768,2,1024]{2,0,1:T(8,128)(2,1)} fusion(bf16[2,2048,4096]{2,1,0:T(8,128)(2,1)} %refs_0_.7, s32[2048]{0:T(1024)S(1)} %iota_add_fusion.1, s32[768]{0:T(1024)S(1)} %get-tuple-element.14, s32[768]{0:T(1024)S(1)} %get-tuple-element.13), kind=kOutput, calls=%fused_computation.99 | convolution fusion | flops 6453460992 | bytes 11548672 | tf_op jit(solution)/shard_map/nr,prc->pnc/dot_general | solution.py:148
  33.9 32.0 %fusion.45 = bf16[768,2,2048]{2,0,1:T(8,128)(2,1)S(1)} fusion(bf16[2,2048,4096]{2,1,0:T(8,128)(2,1)} %refs_0_.7, bf16[4096,768]{0,1:T(8,128)(2,1)} %subtract_convert_fusion), kind=kOutput, calls=%fused_computation.54 | convolution fusion | flops 25772949504 | bytes 46137344 | tf_op jit(solution)/shard_map/prc,cn->prn/dot_general | solution.py:157
  68.6 6.7 %convert_bitcast_fusion.1 = bf16[2,768,768]{1,2,0:T(8,128)(2,1)} fusion(s32[2048]{0:T(1024)S(1)} %iota_add_fusion.1, s32[768]{0:T(1024)S(1)} %get-tuple-element.14, s32[768]{0:T(1024)S(1)} %get-tuple-element.13, bf16[768,2,2048]{2,0,1:T(8,128)(2,1)S(1)} %fusion.45), kind=kOutput, calls=%fused_computation.90 | convolution fusion | flops 4842455040 | bytes 8665088 | tf_op jit(solution)/shard_map/mr,prn->pmn/dot_general | solution.py:158
  75.4 10.4 %fusion.87 = bf16[768,2,1024]{2,0,1:T(8,128)(2,1)} fusion(bf16[2,2048,4096]{2,1,0:T(8,128)(2,1)} %refs_0_.7, s32[2048]{0:T(1024)S(1)} %iota_add_fusion.1, s32[768]{0:T(1024)S(1)} %get-tuple-element.14, s32[768]{0:T(1024)S(1)} %get-tuple-element.13), kind=kOutput, calls=%fused_computation.98 | convolution fusion | flops 6453460992 | bytes 11548672 | tf_op jit(solution)/shard_map/nr,prc->pnc/dot_general | solution.py:148
  86.1 10.4 %fusion.82 = bf16[768,2,1024]{2,0,1:T(8,128)(2,1)} fusion(bf16[2,2048,4096]{2,1,0:T(8,128)(2,1)} %refs_0_.7, s32[2048]{0:T(1024)S(1)} %iota_add_fusion.1, s32[768]{0:T(1024)S(1)} %get-tuple-element.14, s32[768]{0:T(1024)S(1)} %get-tuple-element.13), kind=kOutput, calls=%fused_computation.97 | convolution fusion | flops 6453460992 | bytes 11548672 | tf_op jit(solution)/shard_map/nr,prc->pnc/dot_general | solution.py:148
  96.6 7.4 %reduce-scatter.11.cloned.1.call-done = bf16[192,1024]{1,0:T(8,128)(2,1)} async-done(((bf16[1536,1024]{1,0:T(8,128)(2,1)}), bf16[192,1024]{1,0:T(8,128)(2,1)}) %reduce-scatter.11.cloned.1.call-update) | async-done | bytes 393232 | tf_op jit(solution)/shard_map/reduce_scatter | solution.py:152
  104.1 82.2 %reduce-scatter.9.cloned.1.call-done = bf16[192,1024]{1,0:T(8,128)(2,1)} async-done(((bf16[1536,1024]{1,0:T(8,128)(2,1)}), bf16[192,1024]{1,0:T(8,128)(2,1)}) %reduce-scatter.9.cloned.1.call-update) | async-done | bytes 393232 | tf_op jit(solution)/shard_map/reduce_scatter | solution.py:152
  188.8 52.9 %all-reduce.2.cloned.1.call-done = bf16[2,768,768]{1,2,0:T(8,128)(2,1)} async-done(((bf16[2,768,768]{1,2,0:T(8,128)(2,1)}), bf16[2,768,768]{1,2,0:T(8,128)(2,1)}) %all-reduce.2.cloned.1.call-update) | async-done | bytes 2359312 | tf_op jit(solution)/shard_map/psum | solution.py:159
  253.8 15.7 %reduce-scatter.7.cloned.1.call-done = bf16[192,1024]{1,0:T(8,128)(2,1)} async-done(((bf16[1536,1024]{1,0:T(8,128)(2,1)}), bf16[192,1024]{1,0:T(8,128)(2,1)}) %reduce-scatter.7.cloned.1.call-update) | async-done | bytes 393232 | tf_op jit(solution)/shard_map/reduce_scatter | solution.py:152
  270.1 28.9 %fusion = f32[768,1536]{1,0:T(8,128)} fusion(f32[768,768]{0,1:T(8,128)} %get-tuple-element.30, f32[768,768]{0,1:T(8,128)} %get-tuple-element.22, f32[768,768]{0,1:T(8,128)} %get-tuple-element.21), kind=kOutput, calls=%fused_computation.2 | convolution fusion | flops 10879893504 | bytes 11796480 | tf_op jit(solution)/shard_map/dot_general | solution.py:95
  298.9 6.2 %copy.6 = f32[768,1536]{0,1:T(8,128)} copy(f32[768,1536]{1,0:T(8,128)} %fusion) | data formatting | bytes 9437184 | tf_op jit(solution)/shard_map/dot_general | solution.py:95
  305.2 9.0 %slice_add_fusion.2 = (f32[768,768]{0,1:T(8,128)}, f32[768,768]{0,1:T(8,128)}, f32[768,768]{0,1:T(8,128)}, f32[768,768]{0,1:T(8,128)}) fusion(f32[768,768]{0,1:T(8,128)} %get-tuple-element.30, f32[768,1536]{0,1:T(8,128)} %copy.6, f32[768,768]{0,1:T(8,128)} %get-tuple-element.22), kind=kLoop, calls=%fused_computation.121 | loop fusion | flops 2359296 | bytes 18874368 | tf_op jit(solution)/shard_map/add | solution.py:119
  315.2 15.4 %fusion.8 = f32[768,1536]{0,1:T(8,128)} fusion(f32[768,1536]{1,0:T(8,128)S(1)} %copy-done.6, f32[768,768]{0,1:T(8,128)} %get-tuple-element.34, f32[768,768]{0,1:T(8,128)} %get-tuple-element.32, f32[768,1536]{0,1:T(8,128)S(1)} %copy-done.4), kind=kOutput, calls=%fused_computation.10 | convolution fusion | flops 10876354560 | bytes 18874368 | tf_op jit(solution)/shard_map/dot_general | solution.py:95
  339.3 17.8 %fusion.14 = f32[768,1536]{0,1:T(8,128)S(1)} fusion(f32[768,768]{0,1:T(8,128)} %get-tuple-element.23, f32[768,768]{0,1:T(8,128)} %get-tuple-element.19, f32[768,768]{0,1:T(8,128)} %get-tuple-element.20, f32[768,768]{0,1:T(8,128)} %get-tuple-element.33, f32[768,768]{0,1:T(8,128)} %get-tuple-element.31), kind=kOutput, calls=%fused_computation.16 | convolution fusion | flops 10879893504 | bytes 16515072 | tf_op jit(solution)/shard_map/dot_general | solution.py:95
  358.4 21.2 %maximum_bitcast_fusion.2 = (bf16[1,1536,1536]{1,2,0:T(8,128)(2,1)}, bf16[1,1536,1536]{1,2,0:T(8,128)(2,1)}) fusion(bf16[768,768]{0,1:T(8,128)(2,1)S(1)} %get-tuple-element.17, bf16[768,768]{0,1:T(8,128)(2,1)S(1)} %get-tuple-element.28, bf16[768,1536]{0,1:T(8,128)(2,1)S(1)} %maximum_convert_fusion, bf16[768,768]{0,1:T(8,128)(2,1)S(1)} %get-tuple-element.18, ...), kind=kLoop, calls=%fused_computation.52 | loop fusion | flops 28311552 | bytes 16515072 | tf_op jit(solution)/shard_map/stack | solution.py:130
  386.1 26.2 %convert_bitcast_fusion.refs_1_ = bf16[2,2048,1536]{2,1,0:T(8,128)(2,1)} fusion(bf16[1,1536,1536]{1,2,0:T(8,128)(2,1)} %get-tuple-element.36, bf16[1,1536,1536]{1,2,0:T(8,128)(2,1)S(1)} %bitcast.91, bf16[2048,768]{0,1:T(8,128)(2,1)} %get-tuple-element.25, bf16[2048,768]{0,1:T(8,128)(2,1)} %get-tuple-element.24), kind=kOutput, calls=%fused_computation | convolution fusion | flops 19350945792 | bytes 28311552 | tf_op jit(solution)/shard_map/rk,pkn->prn/dot_general | solution.py:165
  414.2 17.7 %shard_map.28.refs_3_ = bf16[2,2048,4096]{2,1,0:T(8,128)(2,1)} custom-call(bf16[2,2048,4096]{2,1,0:T(8,128)(2,1)} %refs_0_.7, bf16[2,2048,1536]{2,1,0:T(8,128)(2,1)} %convert_bitcast_fusion.refs_1_, bf16[1536,1024]{1,0:T(8,128)(2,1)S(1)} %copy-done), custom_call_target="tpu_custom_call" | custom-call | flops 12884901888 | bytes 32505856 | tf_op jit(solution)/shard_map/pallas_call | solution.py:74
  431.9 38.5 %all-gather.9.cloned.1.call-done.refs_2_ = bf16[1536,1024]{1,0:T(8,128)(2,1)} async-done(((bf16[192,1024]{1,0:T(8,128)(2,1)}), bf16[1536,1024]{1,0:T(8,128)(2,1)}) %all-gather.9.cloned.1.call-update) | async-done | bytes 3145744 | tf_op jit(solution)/shard_map/all_gather | solution.py:168
  472.2 17.6 %shard_map.29.refs_3_ = bf16[2,2048,4096]{2,1,0:T(8,128)(2,1)} custom-call(bf16[2,2048,4096]{2,1,0:T(8,128)(2,1)} %refs_0_.7, bf16[2,2048,1536]{2,1,0:T(8,128)(2,1)} %convert_bitcast_fusion.refs_1_, bf16[1536,1024]{1,0:T(8,128)(2,1)S(1)} %copy-done.1, bf16[2,2048,4096]{2,1,0:T(8,128)(2,1)} %shard_map.28.refs_3_), custom_call_target="tpu_custom_call", output_to_operand_aliasing={{}: (3, {})} | custom-call | flops 12884901888 | bytes 32505856 | tf_op jit(solution)/shard_map/pallas_call | solution.py:74
  489.8 42.0 %all-gather.7.cloned.1.call-done.refs_2_ = bf16[1536,1024]{1,0:T(8,128)(2,1)} async-done(((bf16[192,1024]{1,0:T(8,128)(2,1)}), bf16[1536,1024]{1,0:T(8,128)(2,1)}) %all-gather.7.cloned.1.call-update) | async-done | bytes 3145744 | tf_op jit(solution)/shard_map/all_gather | solution.py:168
  533.7 17.9 %shard_map.30.refs_3_ = bf16[2,2048,4096]{2,1,0:T(8,128)(2,1)} custom-call(bf16[2,2048,4096]{2,1,0:T(8,128)(2,1)} %refs_0_.7, bf16[2,2048,1536]{2,1,0:T(8,128)(2,1)} %convert_bitcast_fusion.refs_1_, bf16[1536,1024]{1,0:T(8,128)(2,1)S(1)} %copy-done.2, bf16[2,2048,4096]{2,1,0:T(8,128)(2,1)} %shard_map.29.refs_3_), custom_call_target="tpu_custom_call", output_to_operand_aliasing={{}: (3, {})} | custom-call | flops 12884901888 | bytes 32505856 | tf_op jit(solution)/shard_map/pallas_call | solution.py:74
  551.6 41.7 %all-gather.5.cloned.1.call-done.refs_2_ = bf16[1536,1024]{1,0:T(8,128)(2,1)} async-done(((bf16[192,1024]{1,0:T(8,128)(2,1)}), bf16[1536,1024]{1,0:T(8,128)(2,1)}) %all-gather.5.cloned.1.call-update) | async-done | bytes 3145744 | tf_op jit(solution)/shard_map/all_gather | solution.py:168
  595.3 17.6 %shard_map.31 = bf16[2,2048,4096]{2,1,0:T(8,128)(2,1)} custom-call(bf16[2,2048,4096]{2,1,0:T(8,128)(2,1)} %refs_0_.7, bf16[2,2048,1536]{2,1,0:T(8,128)(2,1)} %convert_bitcast_fusion.refs_1_, bf16[1536,1024]{1,0:T(8,128)(2,1)S(1)} %copy-done.3, bf16[2,2048,4096]{2,1,0:T(8,128)(2,1)} %shard_map.30.refs_3_), custom_call_target="tpu_custom_call", output_to_operand_aliasing={{}: (3, {})} | custom-call | flops 12884901888 | bytes 32505856 | tf_op jit(solution)/shard_map/pallas_call | solution.py:74
  (65 shorter events, 49.1 us)
Async XLA Ops:
  7.4 96.7 %reduce-scatter.11.cloned.1.call-start = ((), (), s32[]{:S(2)}) async-start(), calls=%async_computation.11 | async-start | bytes 3538944 | tf_op jit(solution)/shard_map/reduce_scatter | solution.py:152
  23.2 163.1 %reduce-scatter.9.cloned.1.call-start = ((), (), s32[]{:S(2)}) async-start(), calls=%async_computation.9 | async-start | bytes 3538944 | tf_op jit(solution)/shard_map/reduce_scatter | solution.py:152
  33.6 208.0 %all-reduce.2.cloned.1.call-start = ((), (), s32[]{:S(2)}) async-start(), calls=%async_computation.4 | async-start | bytes 4718592 | tf_op jit(solution)/shard_map/psum | solution.py:159
  65.9 2.7 copy-start.5
  75.3 194.2 %reduce-scatter.7.cloned.1.call-start = ((), (), s32[]{:S(2)}) async-start(), calls=%async_computation.7 | async-start | bytes 3538944 | tf_op jit(solution)/shard_map/reduce_scatter | solution.py:152
  85.8 293.7 %reduce-scatter.5.cloned.1.call-start = ((), (), s32[]{:S(2)}) async-start(), calls=%async_computation.5 | async-start | bytes 3538944 | tf_op jit(solution)/shard_map/reduce_scatter | solution.py:152
  96.5 315.7 %all-gather.11.cloned.1.call-start = ((), (), s32[]{:S(2)}) async-start(), calls=%async_computation.12 | async-start | bytes 3538944 | tf_op jit(solution)/shard_map/all_gather | solution.py:168
  104.1 366.3 %all-gather.9.cloned.1.call-start = ((), (), s32[]{:S(2)}) async-start(), calls=%async_computation.10 | async-start | bytes 3538944 | tf_op jit(solution)/shard_map/all_gather | solution.py:168
  186.3 345.5 %all-gather.7.cloned.1.call-start = ((), (), s32[]{:S(2)}) async-start(), calls=%async_computation.8 | async-start | bytes 3538944 | tf_op jit(solution)/shard_map/all_gather | solution.py:168
  188.7 55.0 %collective-permute-start = (bf16[2,1024,768]{1,2,0:T(8,128)(2,1)S(1)}, bf16[2,1024,768]{1,2,0:T(8,128)(2,1)}, u32[]{:S(2)}, u32[]{:S(2)}) collective-permute-start(bf16[2,1024,768]{1,2,0:T(8,128)(2,1)S(1)} %dynamic-slice_bitcast_fusion), channel_id=1, source_target_pairs={{0,1},{1,0},{2,3},{3,2},{4,5},{5,4},{6,7},{7,6},{8,9},{9,8},{10,11... | collective-permute-start | bytes 9437192 | tf_op jit(solution)/shard_map/ppermute | solution.py:35
  248.2 82.5 %collective-permute-start.1 = (bf16[2,1024,768]{1,2,0:T(8,128)(2,1)S(1)}, bf16[2,1024,768]{1,2,0:T(8,128)(2,1)}, u32[]{:S(2)}, u32[]{:S(2)}) collective-permute-start(bf16[2,1024,768]{1,2,0:T(8,128)(2,1)S(1)} %bitcast_add_fusion), channel_id=1, source_target_pairs={{0,2},{1,3},{2,0},{3,1},{4,6},{5,7},{6,4},{7,5},{8,10},{9,11},{10,... | collective-permute-start | bytes 9437192 | tf_op jit(solution)/shard_map/ppermute | solution.py:38
  269.5 323.8 %all-gather.5.cloned.1.call-start = ((), (), s32[]{:S(2)}) async-start(), calls=%async_computation.6 | async-start | bytes 3538944 | tf_op jit(solution)/shard_map/all_gather | solution.py:168
  305.2 9.0 %copy-start.4 = (f32[768,1536]{0,1:T(8,128)S(1)}, f32[768,1536]{0,1:T(8,128)}, u32[]{:S(2)}) copy-start(f32[768,1536]{0,1:T(8,128)} %copy.6) | copy-start | bytes 14155780
  305.2 10.0 %copy-start.6 = (f32[768,1536]{1,0:T(8,128)S(1)}, f32[768,1536]{1,0:T(8,128)}, u32[]{:S(2)}) copy-start(f32[768,1536]{1,0:T(8,128)} %fusion) | copy-start | bytes 14155780
  330.6 5.3 copy-start.7
  335.9 43.7 %collective-permute-start.2 = (bf16[2,1024,768]{1,2,0:T(8,128)(2,1)}, bf16[2,1024,768]{1,2,0:T(8,128)(2,1)}, u32[]{:S(2)}, u32[]{:S(2)}) collective-permute-start(bf16[2,1024,768]{1,2,0:T(8,128)(2,1)} %add.112), channel_id=1, source_target_pairs={{0,1},{1,0},{2,3},{3,2},{4,5},{5,4},{6,7},{7,6},{8,9},{9,8},{10,11... | collective-permute-start | bytes 9437192 | tf_op jit(solution)/shard_map/ppermute | solution.py:40
  379.6 6.5 %slice-start = ((s8[4718592]{0:T(1024)(128)(4,1)}), s8[4194304]{0:T(1024)(128)(4,1)S(1)}, s32[]{:S(2)}) async-start(s8[4718592]{0:T(1024)(128)(4,1)} %bitcast.90), calls=%async_computation.13 | async-start | bytes 8388608
  383.0 3.1 slice-start.1
  412.3 1.9 copy-start
  470.3 1.9 copy-start.1
  531.8 1.9 copy-start.2
  593.4 1.9 copy-start.3
Sparse Core Ops, SparseCore 0:
  23.3 80.6 reduce-scatter.10
  108.0 78.2 reduce-scatter.8
  190.3 79.1 reduce-scatter.6
  273.4 73.4 reduce-scatter.4
  349.1 59.7 all-gather.10
  411.2 59.0 all-gather.8
  472.7 59.0 all-gather.6
  534.3 59.0 all-gather.4
Sparse Core Ops, SparseCore 1:
  75.4 166.2 all-reduce.1

commit v2 on v1

--- a/solution.py
+++ b/solution.py
@@ -53,12 +53,12 @@
         o_ref[p] = (y_ref[p].astype(F32) - c).astype(BF)
 
 
-def final_chunk(y, u, w, prev, index):
+def final_chunk(y, u, w, prev, offset):
     _, rows, cols = y.shape
     depth, width = w.shape
     bm = min(512, rows)
-    bn = min(1024, width)
-    base = index * (width // bn)
+    bn = 1024 if width % 1024 == 0 else width
+    base = offset // bn
     first = prev is None
     in_specs = [
         pl.BlockSpec((2, bm, bn), lambda j, i: (0, i, base + j)),
@@ -87,12 +87,13 @@
     )(*args)
 
 
-def times(a_r, a_i, b_r, b_i, precision=lax.Precision.HIGH):
+def times(a_r, a_i, b_r, b_i):
+    a_r, a_i, b_r, b_i = (x.astype(BF) for x in (a_r, a_i, b_r, b_i))
     left = jnp.concatenate([a_r, a_i], axis=1)
     right = jnp.concatenate(
         [jnp.concatenate([b_r, b_i], axis=1), jnp.concatenate([-b_i, b_r], axis=1)], axis=0
     )
-    out = jnp.dot(left, right, precision=precision, preferred_element_type=F32)
+    out = jnp.dot(left, right, preferred_element_type=F32)
     n = b_r.shape[1]
     return out[:, :n], out[:, n:]
 
@@ -140,33 +141,24 @@
     col_table = signed_table(body_dof, cav_dof, col_index * tile_cols, tile_cols)
     row_table = signed_table_t(body_dof, cav_dof, row_index * tile_rows, tile_rows)
 
-    chunks = 4 if tile_cols % 512 == 0 else 1
-    width = tile_cols // chunks
-
-    def row_chunk(j, table):
-        part = receptance[:, :, j * width : (j + 1) * width]
-        terms = jnp.einsum("nr,prc->pnc", table, part, preferred_element_type=F32).astype(BF)
-        return terms.reshape(2 * count, width)
-
-    def scatter(terms):
-        return lax.psum_scatter(terms, "row", scatter_dimension=0, tiled=True)
-
-    rows = row_chunk(0, row_table)
+    rows = jnp.einsum("nr,prc->pnc", row_table, receptance, preferred_element_type=F32).astype(BF)
+    rows = rows.reshape(2 * count, tile_cols)
     col_table, rows = lax.optimization_barrier((col_table, rows))
-    scattered = [scatter(rows)]
+    rhs = lax.psum_scatter(rows, "row", scatter_dimension=0, tiled=True)
     col_terms = jnp.einsum("prc,cn->prn", receptance, col_table, preferred_element_type=F32).astype(BF)
     inter_terms = jnp.einsum("mr,prn->pmn", row_table, col_terms, preferred_element_type=F32).astype(BF)
     interface = lax.psum(inter_terms, ("row", "col"))
-    scattered += [scatter(row_chunk(j, row_table)) for j in range(1, chunks)]
     left = sum_over_col(col_terms, col_size)
     z = interface.astype(F32)
     pages = solve_operator(z[0], z[1])
     left = jnp.concatenate([left[0], left[1]], axis=1)
     u = jnp.einsum("rk,pkn->prn", left, pages, preferred_element_type=F32).astype(BF)
+    cut = tile_cols - tile_cols // 4 if tile_cols % 512 == 0 else tile_cols
     out = None
-    for j in range(chunks):
-        piece = lax.all_gather(scattered[j], "row", axis=0, tiled=True)
-        out = final_chunk(receptance, u, piece, out, j)
+    for start, stop in ((0, cut), (cut, tile_cols)):
+        if stop > start:
+            piece = lax.all_gather(rhs[:, start:stop], "row", axis=0, tiled=True)
+            out = final_chunk(receptance, u, piece, out, start)
     return out
 
 

time: 626 us -> 636 us (1.016)
  waiting for transfers between devices: 281 us -> 387 us
  matrix products: 168 us -> 108 us
  other arithmetic: 61.7 us -> 41.5 us
  local copies, waits for them, and re-layouts: 20.6 us -> 11.7 us
    all_gather x4 -> x2, waiting for transfers between devices: 122 us -> 0.01 us  [local(): piece = lax.all_gather(rhs[:, start:stop], 'row', axis=0, tiled=True)]
    psum x1, waiting for transfers between devices: 52.9 us -> 153 us  [local(): interface = lax.psum(inter_terms, ('row', 'col'))]
    reduce_scatter x4 -> x1, waiting for transfers between devices: 105 us -> 176 us  [local(): rhs = lax.psum_scatter(rows, 'row', scatter_dimension=0, tiled=True)]
    dot_general x7 -> x4, matrix products: 104 us -> 43.6 us  [the longest x1 31.9 us: local(): jnp.einsum('nr,prc->pnc', row_table, receptance, preferred_element_type=F32)]
    ppermute x1, waiting for transfers between devices: 0.01 us -> 58.1 us  [sum_over_col(): lax.ppermute(mine, 'col', [(i, i ^ step) for i in range(size)])]
    add x1 -> x0, other arithmetic: 9 us -> none  [solve_operator(): p_r, p_i = times(a_r + s_r, a_i + s_i, one + s_r + q_r, s_i + q_i)]
    unnamed x20 -> x4, local copies, waits for them, and re-layouts: 11.3 us -> 4.53 us
    pallas_call x4 -> x2, Pallas kernels: 70.8 us -> 65.9 us  [final_chunk(): pl.pallas_call(functools.partial(final_kernel, first), grid=(width // bn,...]
  transfers between devices with their start and end apart: 12 -> 7, of which waited for: 7 -> 3; matrix products, arithmetic and copies ran while one was open for 36% -> 19% of each run, Pallas kernels for 9% -> 8%
where the time goes in v2:
time: 636 us; the launch traced here: 631 us
  waiting for transfers between devices  387 us (61%)
  matrix products  108 us (17%)
  Pallas kernels  65.9 us (10%)
  other arithmetic  41.5 us (7%)
  between operations  15 us (2%)
  local copies, waits for them, and re-layouts  11.7 us (2%)
    reduce_scatter x1, waiting for transfers between devices, local(): rhs = lax.psum_scatter(rows, 'row', scatter_dimension=0, tiled=True)  176 us
    psum x1, waiting for transfers between devices, local(): interface = lax.psum(inter_terms, ('row', 'col'))  153 us
    pallas_call x2, Pallas kernels, final_chunk(): pl.pallas_call(functools.partial(final_kernel, first), grid=(width // bn,...  65.9 us
    ppermute x1, waiting for transfers between devices, sum_over_col(): lax.ppermute(mine, 'col', [(i, i ^ step) for i in range(size)])  58.1 us
    dot_general x1, matrix products, local(): jnp.einsum('prc,cn->prn', receptance, col_table, preferred_element_type=F32)  32.1 us
    dot_general x1, matrix products, local(): jnp.einsum('nr,prc->pnc', row_table, receptance, preferred_element_type=F32)  31.9 us
    dot_general x1, matrix products, local(): jnp.einsum('rk,pkn->prn', left, pages, preferred_element_type=F32)  25.4 us
    another operation x1, other arithmetic, solve_operator(): return jnp.stack([first, second]).astype(BF)  21.2 us
  transfers between devices with their start and end apart: 7, of which 3 were waited for; matrix products, arithmetic and copies ran while one was open for 19% of the time, Pallas kernels for 8%

profile of v2, /device:TPU:0, one launch (start us, length us, event | category | flops | bytes accessed | tf_op | source)
XLA Modules:
  0.0 631.5 jit_solution(15564661384411539120)
XLA Ops:
  8.2 4.7 subtract_convert_fusion
  12.8 31.9 %convolution_convert_fusion = bf16[768,2,4096]{2,0,1:T(8,128)(2,1)} fusion(bf16[2,2048,4096]{2,1,0:T(8,128)(2,1)} %refs_0_.3, s32[2048]{0:T(1024)S(1)} %iota_add_fusion.1, s32[768]{0:T(1024)S(1)} %get-tuple-element.14, s32[768]{0:T(1024)S(1)} %get-tuple-element.13), kind=kOutput, calls=%fused_computation.5 | convolution fusion | flops 25785532416 | bytes 46151680 | tf_op jit(solution)/shard_map/nr,prc->pnc/dot_general | solution.py:144
  45.3 32.1 %fusion.33 = bf16[768,2,2048]{2,0,1:T(8,128)(2,1)S(1)} fusion(bf16[2,2048,4096]{2,1,0:T(8,128)(2,1)} %refs_0_.3, bf16[4096,768]{0,1:T(8,128)(2,1)} %subtract_convert_fusion), kind=kOutput, calls=%fused_computation.43 | convolution fusion | flops 25772949504 | bytes 46137344 | tf_op jit(solution)/shard_map/prc,cn->prn/dot_general | solution.py:148
  77.4 2.6 copy-done.1
  80.0 6.7 %convert_bitcast_fusion.1 = bf16[2,768,768]{1,2,0:T(8,128)(2,1)} fusion(s32[2048]{0:T(1024)S(1)} %iota_add_fusion.1, s32[768]{0:T(1024)S(1)} %get-tuple-element.14, s32[768]{0:T(1024)S(1)} %get-tuple-element.13, bf16[768,2,2048]{2,0,1:T(8,128)(2,1)S(1)} %fusion.33), kind=kOutput, calls=%fused_computation.83 | convolution fusion | flops 4842455040 | bytes 8665088 | tf_op jit(solution)/shard_map/mr,prn->pmn/dot_general | solution.py:149
  86.8 175.9 %reduce-scatter.2.cloned.1.call-done = bf16[192,4096]{1,0:T(8,128)(2,1)} async-done(((bf16[1536,4096]{1,0:T(8,128)(2,1)}), bf16[192,4096]{1,0:T(8,128)(2,1)}) %reduce-scatter.2.cloned.1.call-update) | async-done | bytes 1572880 | tf_op jit(solution)/shard_map/reduce_scatter | solution.py:147
  262.7 2.4 slice.67
  265.4 2.2 dynamic-slice_bitcast_fusion
  267.7 153.1 %all-reduce.2.cloned.1.call-done = bf16[2,768,768]{1,2,0:T(8,128)(2,1)} async-done(((bf16[2,768,768]{1,2,0:T(8,128)(2,1)}), bf16[2,768,768]{1,2,0:T(8,128)(2,1)}) %all-reduce.2.cloned.1.call-update) | async-done | bytes 2359312 | tf_op jit(solution)/shard_map/psum | solution.py:150
  420.8 2.0 convert_element_type.90
  422.8 4.4 bitcast_add_fusion
  430.2 3.9 fusion.9
  434.4 3.9 fusion.17
  438.3 58.1 %collective-permute-done.1 = bf16[2,1024,768]{1,2,0:T(8,128)(2,1)S(1)} collective-permute-done((bf16[2,1024,768]{1,2,0:T(8,128)(2,1)S(1)}, bf16[2,1024,768]{1,2,0:T(8,128)(2,1)S(1)}, u32[]{:S(2)}, u32[]{:S(2)}) %collective-permute-start.1) | collective-permute-done | bytes 3145760 | tf_op jit(solution)/shard_map/ppermute | solution.py:38
  496.5 1.6 add.106
  498.1 2.0 add_convert_fusion.1
  500.4 3.9 fusion.25
  505.7 21.2 %maximum_bitcast_fusion.2 = (bf16[1,1536,1536]{1,2,0:T(8,128)(2,1)}, bf16[1,1536,1536]{1,2,0:T(8,128)(2,1)}) fusion(bf16[768,768]{0,1:T(8,128)(2,1)S(1)} %get-tuple-element.17, bf16[768,768]{0,1:T(8,128)(2,1)S(1)} %get-tuple-element.31, bf16[768,1536]{0,1:T(8,128)(2,1)S(1)} %maximum_convert_fusion, bf16[768,768]{0,1:T(8,128)(2,1)S(1)} %get-tuple-element.18, ...), kind=kLoop, calls=%fused_computation.41 | loop fusion | flops 28311552 | bytes 16515072 | tf_op jit(solution)/shard_map/stack | solution.py:131
  527.3 2.0 fusion.40
  529.2 1.8 slice.66
  531.0 25.4 %convert_bitcast_fusion.refs_1_ = bf16[2,2048,1536]{2,1,0:T(8,128)(2,1)} fusion(bf16[1,1536,1536]{1,2,0:T(8,128)(2,1)} %get-tuple-element.36, bf16[1,1536,1536]{1,2,0:T(8,128)(2,1)} %get-tuple-element.35, bf16[2048,768]{0,1:T(8,128)(2,1)} %get-tuple-element.28, bf16[2048,768]{0,1:T(8,128)(2,1)S(1)} %get-tuple-element.27), kind=kOutput, calls=%fused_computation | convolution fusion | flops 19350945792 | bytes 28311552 | tf_op jit(solution)/shard_map/rk,pkn->prn/dot_general | solution.py:155
  556.4 48.3 %shard_map.28.refs_3_ = bf16[2,2048,4096]{2,1,0:T(8,128)(2,1)} custom-call(bf16[2,2048,4096]{2,1,0:T(8,128)(2,1)} %refs_0_.3, bf16[2,2048,1536]{2,1,0:T(8,128)(2,1)} %convert_bitcast_fusion.refs_1_, bf16[1536,3072]{1,0:T(8,128)(2,1)} %all-gather.5.cloned.1.call-done.refs_2_), custom_call_target="tpu_custom_call" | custom-call | flops 38654705664 | bytes 72351744 | tf_op jit(solution)/shard_map/pallas_call | solution.py:74
  604.7 1.9 copy-done
  606.6 17.6 %shard_map.29 = bf16[2,2048,4096]{2,1,0:T(8,128)(2,1)} custom-call(bf16[2,2048,4096]{2,1,0:T(8,128)(2,1)} %refs_0_.3, bf16[2,2048,1536]{2,1,0:T(8,128)(2,1)} %convert_bitcast_fusion.refs_1_, bf16[1536,1024]{1,0:T(8,128)(2,1)S(1)} %copy-done, bf16[2,2048,4096]{2,1,0:T(8,128)(2,1)} %shard_map.28.refs_3_), custom_call_target="tpu_custom_call", output_to_operand_aliasing={{}: (3, {})} | custom-call | flops 12884901888 | bytes 32505856 | tf_op jit(solution)/shard_map/pallas_call | solution.py:74
  (31 shorter events, 7.1 us)
Async XLA Ops:
  7.4 255.3 %reduce-scatter.2.cloned.1.call-start = ((), (), s32[]{:S(2)}) async-start(), calls=%async_computation.2 | async-start | bytes 14155776 | tf_op jit(solution)/shard_map/reduce_scatter | solution.py:147
  44.8 376.0 %all-reduce.2.cloned.1.call-start = ((), (), s32[]{:S(2)}) async-start(), calls=%async_computation.1 | async-start | bytes 4718592 | tf_op jit(solution)/shard_map/psum | solution.py:150
  77.4 2.7 copy-start.1
  86.7 469.7 %all-gather.5.cloned.1.call-start = ((), (), s32[]{:S(2)}) async-start(), calls=%async_computation.4 | async-start | bytes 10616832 | tf_op jit(solution)/shard_map/all_gather | solution.py:160
  265.1 339.5 %all-gather.3.cloned.1.call-start = ((), (), s32[]{:S(2)}) async-start(), calls=%async_computation.3 | async-start | bytes 3538944 | tf_op jit(solution)/shard_map/all_gather | solution.py:160
  267.6 155.2 %collective-permute-start = (bf16[2,1024,768]{1,2,0:T(8,128)(2,1)S(1)}, bf16[2,1024,768]{1,2,0:T(8,128)(2,1)}, u32[]{:S(2)}, u32[]{:S(2)}) collective-permute-start(bf16[2,1024,768]{1,2,0:T(8,128)(2,1)S(1)} %dynamic-slice_bitcast_fusion), channel_id=1, source_target_pairs={{0,1},{1,0},{2,3},{3,2},{4,5},{5,4},{6,7},{7,6},{8,9},{9,8},{10,11... | collective-permute-start | bytes 9437192 | tf_op jit(solution)/shard_map/ppermute | solution.py:35
  427.2 69.2 %collective-permute-start.1 = (bf16[2,1024,768]{1,2,0:T(8,128)(2,1)S(1)}, bf16[2,1024,768]{1,2,0:T(8,128)(2,1)S(1)}, u32[]{:S(2)}, u32[]{:S(2)}) collective-permute-start(bf16[2,1024,768]{1,2,0:T(8,128)(2,1)S(1)} %bitcast_add_fusion), channel_id=1, source_target_pairs={{0,2},{1,3},{2,0},{3,1},{4,6},{5,7},{6,4},{7,5},{8,10},{9,11},{10,... | collective-permute-start | bytes 9437192 | tf_op jit(solution)/shard_map/ppermute | solution.py:38
  498.0 28.8 %collective-permute-start.2 = (bf16[2,1024,768]{1,2,0:T(8,128)(2,1)S(1)}, bf16[2,1024,768]{1,2,0:T(8,128)(2,1)S(1)}, u32[]{:S(2)}, u32[]{:S(2)}) collective-permute-start(bf16[2,1024,768]{1,2,0:T(8,128)(2,1)S(1)} %add.106), channel_id=1, source_target_pairs={{0,1},{1,0},{2,3},{3,2},{4,5},{5,4},{6,7},{7,6},{8,9},{9,8},{10,11... | collective-permute-start | bytes 9437192 | tf_op jit(solution)/shard_map/ppermute | solution.py:40
  604.7 1.9 copy-start
Sparse Core Ops, SparseCore 0:
  44.9 217.7 reduce-scatter.1
  265.3 139.5 all-gather.4
  531.2 58.2 all-gather.2
Sparse Core Ops, SparseCore 1:
  86.8 333.9 all-reduce.1
